TPU v7x, 32 devices: a whole 2x2x4 slice. The times are simulated.
32 devices in a mesh: dp: 8 (over y, x, core), seq: 4 (over z).
Axes of the slice: x: 2, y: 2, z: 4, core: 2. Of those that a mesh axis runs over, the one named last changes fastest.
Arguments:
- block_input: bfloat16 [2, 8, 1024, 768], P(None, 'dp', 'seq'), may hold values from -6 to 6
- cotangent: bfloat16 [2, 8, 1024, 768], P(None, 'dp', 'seq'), may hold values from -6 to 6
- segments: int32 [2, 8, 1024], P(None, 'dp'), may hold values from 0 to 3, never falling along the last dimension, each value on 1 to 768 neighbouring positions
- rand_blocks: int32 [12, 16, 3], replicated, may hold values from 0 to 15
- w_attn: float32 [768, 2304], P('dp'), may hold values from -0.21875 to 0.21875
- w_out: float32 [768, 768], P('dp'), may hold values from -1.5 to 1.5
- w_up: float32 [768, 3072], P('dp'), may hold values from -0.21875 to 0.21875
- w_down: float32 [3072, 768], P('dp'), may hold values from -0.109375 to 0.109375
- up_bias: float32 [3072], P('dp'), may hold values from -3 to 3
- bias_rows: float32 [6, 768], P(None, 'dp'), may hold values from -2 to 2
- norm_gains: float32 [2, 768], P(None, 'dp'), may hold values from 0.25 to 1.75
Outputs:
- block_output: bfloat16 [2, 8, 1024, 768], P(None, 'dp', 'seq')
- input_grad: float32 [2, 8, 1024, 768], P(None, 'dp', 'seq')
- grad_w_attn: float32 [768, 2304], P('dp')
- grad_w_out: float32 [768, 768], P('dp')
- grad_w_up: float32 [768, 3072], P('dp')
- grad_w_down: float32 [3072, 768], P('dp')
- grad_up_bias: float32 [3072], P('dp')
- grad_bias_rows: float32 [6, 768], P(None, 'dp')
- grad_norm_gains: float32 [2, 768], P(None, 'dp')
Inputs may be any that keep to these rules, and one draw needn't show every extreme that they name: `segments`: segment numbers never fall along a sequence. `rand_blocks`: block numbers within the sequence.
All inputs are finite; a program needn't handle non-finite values.
Results may differ from a plain program's by a relative error of at most 0.018.
Values may be sent and summed in bfloat16 or wider, within the bound.
No kernel may reach another device: no remote copies, remote signals or barrier semaphores. Data moves between devices by JAX's collectives and lax.ppermute only.
A program may use at most 192 MiB of HBM per device.

v0:
```python
import jax
import jax.numpy as jnp
from jax import lax
from jax.sharding import PartitionSpec as P

EPSILON = 1e-05
MASKED = -1e30


def layer_norm(tensor, gain_row, offset):
    centre = tensor - jnp.mean(tensor, axis=-1, keepdims=True)
    spread = jnp.mean(centre * centre, axis=-1, keepdims=True)
    return centre * lax.rsqrt(spread + EPSILON) * gain_row + offset


def gelu_exact(tensor):
    return jax.nn.gelu(tensor, approximate=False)


def col_sums(tensor):
    return jnp.sum(tensor.astype(jnp.float32), axis=0)


def outer_grad(left, right):
    return lax.dot_general(
        left, right, (((0,), (0,)), ((), ())), preferred_element_type=jnp.float32
    )


def times_transposed(left, right):
    return lax.dot_general(
        left, right, (((1,), (1,)), ((), ())), preferred_element_type=jnp.float32
    )


def cast_half(params):
    return tuple((member.astype(jnp.bfloat16) for member in params))


def visible_mask(rand_blocks, first_row, local_rows, seq_len):
    head_count = rand_blocks.shape[0]
    nblocks = rand_blocks.shape[1]
    block_len = seq_len // nblocks
    local_blocks = local_rows // block_len
    query_block = (first_row + jnp.arange(local_rows, dtype=jnp.int32)) // block_len
    key_block = jnp.arange(seq_len, dtype=jnp.int32) // block_len
    nearby = jnp.abs(query_block[:, None] - key_block[None, :]) <= 1
    global_q = (query_block == 0) | (query_block == nblocks - 1)
    global_k = (key_block == 0) | (key_block == nblocks - 1)
    always = nearby | global_q[:, None] | global_k[None, :]
    chosen = lax.dynamic_slice_in_dim(rand_blocks, first_row // block_len, local_blocks, 1)
    block_ids = jnp.arange(nblocks, dtype=jnp.int32)
    random_hit = jnp.any(chosen[:, :, :, None] == block_ids[None, None, None, :], axis=2)
    random_hit = jnp.broadcast_to(
        random_hit[:, :, None, :, None], (head_count, local_blocks, block_len, nblocks, block_len)
    )
    return always[None] | random_hit.reshape(head_count, local_rows, seq_len)


def score_block(query_heads, key_heads, allowed, score_scale):
    scores = (
        jnp.einsum("sqhd,skhd->shqk", query_heads, key_heads, preferred_element_type=jnp.float32)
        * score_scale
    )
    return jnp.where(allowed, scores, MASKED)


def forward_pass(tokens, seg_full, weights, mask_blocks, first_row):
    w_attn_b, w_out_b, w_up_b, w_down_b, up_bias_b, bias_b, gain_b = weights
    seq_count, local_rows, model_width = tokens.shape
    head_count = mask_blocks.shape[0]
    head_size = model_width // head_count
    score_scale = head_size ** (-0.5)
    bias_f = bias_b.astype(jnp.float32)
    gain_f = gain_b.astype(jnp.float32)
    row_data = tokens.reshape(-1, model_width)
    projected = jnp.dot(row_data, w_attn_b, preferred_element_type=jnp.float32)
    queries = (projected[:, :model_width] + bias_f[0]).astype(jnp.bfloat16)
    keys_loc = projected[:, model_width : 2 * model_width].astype(jnp.bfloat16)
    values_loc = (projected[:, 2 * model_width :] + bias_f[1]).astype(jnp.bfloat16)
    keys_full, values_full = (
        lax.all_gather(
            keys_loc.reshape(seq_count, local_rows, model_width), "seq", axis=1, tiled=True
        ),
        lax.all_gather(
            values_loc.reshape(seq_count, local_rows, model_width), "seq", axis=1, tiled=True
        ),
    )
    seq_len = keys_full.shape[1]
    query_heads = queries.reshape(seq_count, local_rows, head_count, head_size)
    key_heads = keys_full.reshape(seq_count, seq_len, head_count, head_size)
    value_heads = values_full.reshape(seq_count, seq_len, head_count, head_size)
    seg_local = lax.dynamic_slice_in_dim(seg_full, first_row, local_rows, 1)
    allowed = mask_blocks[None] & (seg_local[:, None, :, None] == seg_full[:, None, None, :])
    scores = score_block(query_heads, key_heads, allowed, score_scale)
    row_max = jnp.max(scores, axis=-1, keepdims=True)
    exponent = jnp.exp(scores - row_max)
    row_total = jnp.sum(exponent, axis=-1, keepdims=True)
    attn_probs = exponent / row_total
    log_total = row_max + jnp.log(row_total)
    probs_low = attn_probs.astype(jnp.bfloat16)
    mixture = jnp.einsum(
        "shqk,skhd->sqhd", probs_low, value_heads, preferred_element_type=jnp.float32
    )
    attended = mixture.reshape(-1, model_width).astype(jnp.bfloat16)
    branch = jnp.dot(attended, w_out_b, preferred_element_type=jnp.float32) + bias_f[2]
    first_norm, first_back = jax.vjp(
        layer_norm, row_data.astype(jnp.float32) + branch, gain_f[0], bias_f[4]
    )
    first_low = first_norm.astype(jnp.bfloat16)
    pre_act = jnp.dot(first_low, w_up_b, preferred_element_type=jnp.float32) + up_bias_b.astype(
        jnp.float32
    )
    act_float, gelu_back = jax.vjp(gelu_exact, pre_act)
    activation = act_float.astype(jnp.bfloat16)
    ffn_out = jnp.dot(activation, w_down_b, preferred_element_type=jnp.float32) + bias_f[3]
    result, second_back = jax.vjp(layer_norm, first_norm + ffn_out, gain_f[1], bias_f[5])
    stored = (
        row_data,
        query_heads,
        key_heads,
        value_heads,
        allowed,
        log_total,
        attended,
        first_low,
        activation,
        first_back,
        gelu_back,
        second_back,
    )
    return (result.astype(jnp.bfloat16).reshape(seq_count, local_rows, model_width), stored)


def backward_pass(stored, upstream, weights):
    w_attn_b, w_out_b, w_up_b, w_down_b, up_bias_b, bias_b, gain_b = weights
    (
        row_data,
        query_heads,
        key_heads,
        value_heads,
        allowed,
        log_total,
        attended,
        first_low,
        activation,
        first_back,
        gelu_back,
        second_back,
    ) = stored
    seq_count, local_rows, head_count, head_size = query_heads.shape
    seq_len = key_heads.shape[1]
    model_width = head_count * head_size
    score_scale = head_size ** (-0.5)
    grad_second, grad_gain_two, grad_shift_two = second_back(upstream)
    ffn_grad = grad_second.astype(jnp.bfloat16)
    grad_down = outer_grad(activation, ffn_grad)
    grad_bias_down = col_sums(ffn_grad)
    act_grad = times_transposed(ffn_grad, w_down_b)
    (pre_float,) = gelu_back(act_grad)
    pre_grad = pre_float.astype(jnp.bfloat16)
    grad_up = outer_grad(first_low, pre_grad)
    grad_up_bias = col_sums(pre_grad)
    first_grad = grad_second + times_transposed(pre_grad, w_up_b)
    grad_first, grad_gain_one, grad_shift_one = first_back(first_grad)
    branch_grad = grad_first.astype(jnp.bfloat16)
    grad_out = outer_grad(attended, branch_grad)
    grad_bias_out = col_sums(branch_grad)
    attended_grad = (
        times_transposed(branch_grad, w_out_b)
        .astype(jnp.bfloat16)
        .reshape(seq_count, local_rows, head_count, head_size)
    )
    scores = score_block(query_heads, key_heads, allowed, score_scale)
    attn_probs = jnp.exp(scores - log_total)
    prob_grad = jnp.einsum(
        "sqhd,skhd->shqk", attended_grad, value_heads, preferred_element_type=jnp.float32
    )
    row_dot = jnp.sum(prob_grad * attn_probs, axis=-1, keepdims=True)
    score_grad = (attn_probs * (prob_grad - row_dot)).astype(jnp.bfloat16)
    query_grad = (
        jnp.einsum("shqk,skhd->sqhd", score_grad, key_heads, preferred_element_type=jnp.float32)
        * score_scale
    ).astype(jnp.bfloat16)
    probs_low = attn_probs.astype(jnp.bfloat16)
    value_part = jnp.einsum(
        "shqk,sqhd->skhd", probs_low, attended_grad, preferred_element_type=jnp.float32
    )
    key_part = (
        jnp.einsum("shqk,sqhd->skhd", score_grad, query_heads, preferred_element_type=jnp.float32)
        * score_scale
    )
    key_grad, value_grad = (
        lax.psum_scatter(
            key_part.reshape(seq_count, seq_len, model_width).astype(jnp.bfloat16),
            "seq",
            scatter_dimension=1,
            tiled=True,
        ).astype(jnp.float32),
        lax.psum_scatter(
            value_part.reshape(seq_count, seq_len, model_width).astype(jnp.bfloat16),
            "seq",
            scatter_dimension=1,
            tiled=True,
        ).astype(jnp.float32),
    )
    key_low = key_grad.astype(jnp.bfloat16).reshape(-1, model_width)
    value_low = value_grad.astype(jnp.bfloat16).reshape(-1, model_width)
    query_low = query_grad.reshape(-1, model_width)
    proj_grad = jnp.concatenate([query_low, key_low, value_low], axis=1)
    grad_attn = outer_grad(row_data, proj_grad)
    input_grad = grad_first + times_transposed(proj_grad, w_attn_b)
    grad_biases = jnp.stack(
        [
            col_sums(query_low),
            col_sums(value_low),
            grad_bias_out,
            grad_bias_down,
            grad_shift_one,
            grad_shift_two,
        ]
    )
    grad_gains = jnp.stack([grad_gain_one, grad_gain_two])
    gradients = (grad_attn, grad_out, grad_up, grad_down, grad_up_bias, grad_biases, grad_gains)
    return (input_grad.reshape(seq_count, local_rows, model_width), gradients)


def body(
    block_input,
    cotangent,
    segments,
    rand_blocks,
    w_attn,
    w_out,
    w_up,
    w_down,
    up_bias,
    bias_rows,
    norm_gains,
):
    micro_count, seq_count, local_rows, model_width = block_input.shape
    seq_len = segments.shape[2]
    first_row = lax.axis_index("seq") * local_rows
    mask_blocks = visible_mask(rand_blocks, first_row, local_rows, seq_len)
    masters = (w_attn, w_out, w_up, w_down, up_bias, bias_rows, norm_gains)
    halves = cast_half(masters)
    totals = tuple(
        (
            (
                jnp.zeros((member.shape[0] * lax.axis_size("dp"),) + member.shape[1:], jnp.float32)
                if member.ndim == 1 or (member is not bias_rows and member is not norm_gains)
                else jnp.zeros(
                    (member.shape[0], member.shape[1] * lax.axis_size("dp")), jnp.float32
                )
            )
            for member in masters
        )
    )
    outputs = []
    in_grads = []
    for micro_index in range(micro_count):
        fwd_set = (
            lax.all_gather(halves[0], "dp", axis=0, tiled=True),
            lax.all_gather(halves[1], "dp", axis=0, tiled=True),
            lax.all_gather(halves[2], "dp", axis=0, tiled=True),
            lax.all_gather(halves[3], "dp", axis=0, tiled=True),
            lax.all_gather(halves[4], "dp", axis=0, tiled=True),
            lax.all_gather(halves[5], "dp", axis=1, tiled=True),
            lax.all_gather(halves[6], "dp", axis=1, tiled=True),
        )
        result, stored = forward_pass(
            block_input[micro_index], segments[micro_index], fwd_set, mask_blocks, first_row
        )
        outputs.append(result)
        back_set = (
            lax.all_gather(halves[0], "dp", axis=0, tiled=True),
            lax.all_gather(halves[1], "dp", axis=0, tiled=True),
            lax.all_gather(halves[2], "dp", axis=0, tiled=True),
            lax.all_gather(halves[3], "dp", axis=0, tiled=True),
            lax.all_gather(halves[4], "dp", axis=0, tiled=True),
            lax.all_gather(halves[5], "dp", axis=1, tiled=True),
            lax.all_gather(halves[6], "dp", axis=1, tiled=True),
        )
        upstream = cotangent[micro_index].reshape(-1, model_width).astype(jnp.float32)
        input_grad, gradients = backward_pass(stored, upstream, back_set)
        in_grads.append(input_grad)
        totals = tuple((total_part + grad_part for total_part, grad_part in zip(totals, gradients)))
    shards = (
        lax.psum_scatter(totals[0], "dp", scatter_dimension=0, tiled=True),
        lax.psum_scatter(totals[1], "dp", scatter_dimension=0, tiled=True),
        lax.psum_scatter(totals[2], "dp", scatter_dimension=0, tiled=True),
        lax.psum_scatter(totals[3], "dp", scatter_dimension=0, tiled=True),
        lax.psum_scatter(totals[4], "dp", scatter_dimension=0, tiled=True),
        lax.psum_scatter(totals[5], "dp", scatter_dimension=1, tiled=True),
        lax.psum_scatter(totals[6], "dp", scatter_dimension=1, tiled=True),
    )
    summed = (
        lax.psum(shards[0].astype(jnp.bfloat16), "seq").astype(jnp.float32),
        lax.psum(shards[1].astype(jnp.bfloat16), "seq").astype(jnp.float32),
        lax.psum(shards[2].astype(jnp.bfloat16), "seq").astype(jnp.float32),
        lax.psum(shards[3].astype(jnp.bfloat16), "seq").astype(jnp.float32),
        lax.psum(shards[4].astype(jnp.bfloat16), "seq").astype(jnp.float32),
        lax.psum(shards[5].astype(jnp.bfloat16), "seq").astype(jnp.float32),
        lax.psum(shards[6].astype(jnp.bfloat16), "seq").astype(jnp.float32),
    )
    return (
        jnp.stack(outputs, 0),
        jnp.stack(in_grads, 0),
        summed[0],
        summed[1],
        summed[2],
        summed[3],
        summed[4],
        summed[5],
        summed[6],
    )


def solution(mesh):
    return jax.shard_map(
        body,
        mesh=mesh,
        in_specs=(
            P(None, "dp", "seq", None),
            P(None, "dp", "seq", None),
            P(None, "dp", None),
            P(),
            P("dp", None),
            P("dp", None),
            P("dp", None),
            P("dp", None),
            P("dp"),
            P(None, "dp"),
            P(None, "dp"),
        ),
        out_specs=(
            P(None, "dp", "seq", None),
            P(None, "dp", "seq", None),
            P("dp", None),
            P("dp", None),
            P("dp", None),
            P("dp", None),
            P("dp"),
            P(None, "dp"),
            P(None, "dp"),
        ),
        check_vma=False,
    )
```

profile of v0, /device:TPU:0, one launch (start us, length us, event | category | flops | bytes accessed | tf_op | source)
XLA Modules:
  0.0 952.1 jit_solution(16371674868866285277)
XLA Ops:
  9.3 37.9 %all-gather.16.cloned.1.call-done = bf16[768,2304]{1,0:T(8,128)(2,1)} async-done(((bf16[96,2304]{1,0:T(8,128)(2,1)}), bf16[768,2304]{1,0:T(8,128)(2,1)}) %all-gather.16.cloned.1.call-update) | async-done | bytes 3538960 | tf_op jit(solution)/shard_map/all_gather | solution.py:263
  52.7 8.9 all-gather.4
  72.5 7.9 all-gather.5
  80.5 8.8 all-gather.6
  93.9 17.3 %reshape.625 = pred[12,256,1024]{2,1,0:T(32,128)(4,1)} reshape(pred[12,4,64,16,64]{4,3,2,1,0:T(8,128)(4,1)} %broadcast_in_dim.25) | data formatting | bytes 6291456 | tf_op jit(solution)/shard_map/reshape | solution.py:57
  131.0 6.7 fusion.38
  137.7 15.0 %all-gather.18.cloned.1.call-done = bf16[768,768]{1,0:T(8,128)(2,1)} async-done(((bf16[96,768]{1,0:T(8,128)(2,1)}), bf16[768,768]{1,0:T(8,128)(2,1)}) %all-gather.18.cloned.1.call-update) | async-done | bytes 1179664 | tf_op jit(solution)/shard_map/all_gather | solution.py:264
  154.8 39.1 %all-gather.20.cloned.1.call-done = bf16[768,3072]{1,0:T(8,128)(2,1)} async-done(((bf16[96,3072]{1,0:T(8,128)(2,1)}), bf16[768,3072]{1,0:T(8,128)(2,1)}) %all-gather.20.cloned.1.call-update) | async-done | bytes 4718608 | tf_op jit(solution)/shard_map/all_gather | solution.py:265
  194.0 11.6 %multiply_convert_fusion.4 = (bf16[256,3072]{1,0:T(8,128)(2,1)}, f32[256,3072]{1,0:T(8,128)}, f32[256,3072]{1,0:T(8,128)}) fusion(f32[3072]{0:T(1024)S(1)} %bitcast.239, bf16[768,3072]{1,0:T(8,128)(2,1)} %all-gather.20.cloned.1.call-done, f32[256,768]{1,0:T(8,128)S(1)} %get-tuple-element.135, f32[256]{0:T(256)S(1)} %fusion.79, ...), kind=kOutput, calls=%fused_computation.37 | convolution fusion | flops 1260847104 | bytes 13389824 | tf_op jit(solution)/shard_map/dot_general | solution.py:111
  205.6 29.6 %all-gather.22.cloned.1.call-done = bf16[3072,768]{1,0:T(8,128)(2,1)} async-done(((bf16[384,768]{1,0:T(8,128)(2,1)}), bf16[3072,768]{1,0:T(8,128)(2,1)}) %all-gather.22.cloned.1.call-update) | async-done | bytes 4718608 | tf_op jit(solution)/shard_map/all_gather | solution.py:266
  239.6 34.9 %all-gather.26.cloned.1.call-done = bf16[1024,768]{1,0:T(8,128)(2,1)} async-done(((bf16[256,768]{1,0:T(8,128)(2,1)}), bf16[1024,768]{1,0:T(8,128)(2,1)}) %all-gather.26.cloned.1.call-update) | async-done | bytes 1572880 | tf_op jit(solution)/shard_map/all_gather | solution.py:82
  277.4 6.8 fusion.97
  288.7 23.9 %all-gather.24.cloned.1.call-done = bf16[1024,768]{1,0:T(8,128)(2,1)} async-done(((bf16[256,768]{1,0:T(8,128)(2,1)}), bf16[1024,768]{1,0:T(8,128)(2,1)}) %all-gather.24.cloned.1.call-update) | async-done | bytes 1572880 | tf_op jit(solution)/shard_map/all_gather | solution.py:85
  315.2 6.6 fusion.39
  322.7 11.6 %multiply_convert_fusion.5 = (bf16[256,3072]{1,0:T(8,128)(2,1)S(1)}, f32[256,3072]{1,0:T(8,128)S(1)}, f32[256,3072]{1,0:T(8,128)}) fusion(f32[3072]{0:T(1024)S(1)} %bitcast.240, bf16[768,3072]{1,0:T(8,128)(2,1)} %all-gather.20.cloned.1.call-done, f32[256,768]{1,0:T(8,128)S(1)} %get-tuple-element.128, f32[768]{0:T(1024)S(1)} %get-tuple-element.70, ...), kind=kOutput, calls=%fused_computation.50 | convolution fusion | flops 1260847104 | bytes 13389824 | tf_op jit(solution)/shard_map/dot_general | solution.py:111
  352.8 8.1 fusion.24
  361.0 7.0 multiply_reduce_fusion.1
  383.4 8.0 fusion.27
  391.5 7.2 multiply_reduce_fusion
  436.9 31.9 %reduce-scatter.23.cloned.1.call-done = bf16[1,256,768]{1,2,0:T(8,128)(2,1)} async-done(((bf16[1,1024,768]{1,2,0:T(8,128)(2,1)}), bf16[1,256,768]{1,2,0:T(8,128)(2,1)}) %reduce-scatter.23.cloned.1.call-update) | async-done | bytes 393232 | tf_op jit(solution)/shard_map/reduce_scatter | solution.py:200
  468.8 36.4 %reduce-scatter.21.cloned.1.call-done = bf16[1,256,768]{1,2,0:T(8,128)(2,1)} async-done(((bf16[1,1024,768]{1,2,0:T(8,128)(2,1)}), bf16[1,256,768]{1,2,0:T(8,128)(2,1)}) %reduce-scatter.21.cloned.1.call-update) | async-done | bytes 393232 | tf_op jit(solution)/shard_map/reduce_scatter | solution.py:194
  505.2 7.4 add_bitcast_fusion
  512.6 8.2 copy.84
  541.6 8.5 reduce-scatter.25.cloned.1.call-done
  551.7 67.7 %reduce-scatter.31.cloned.1.call-done = f32[96,2304]{1,0:T(8,128)} async-done(((f32[768,2304]{1,0:T(8,128)}), f32[96,2304]{1,0:T(8,128)}) %reduce-scatter.31.cloned.1.call-update) | async-done | bytes 884752
  621.6 77.6 %reduce-scatter.27.cloned.1.call-done = f32[96,3072]{1,0:T(8,128)} async-done(((f32[768,3072]{1,0:T(8,128)}), f32[96,3072]{1,0:T(8,128)}) %reduce-scatter.27.cloned.1.call-update) | async-done | bytes 1179664 | tf_op jit(solution)/shard_map/reduce_scatter | solution.py:291
  701.4 77.7 %reduce-scatter.29.cloned.1.call-done = f32[384,768]{1,0:T(8,128)} async-done(((f32[3072,768]{1,0:T(8,128)}), f32[384,768]{1,0:T(8,128)}) %reduce-scatter.29.cloned.1.call-update) | async-done | bytes 1179664 | tf_op jit(solution)/shard_map/reduce_scatter | solution.py:292
  782.5 23.1 %all-reduce = bf16[3072]{0:T(1024)(128)(2,1)S(1)} all-reduce(f32[3072]{0:T(1024)S(1)} %add.337), channel_id=14, replica_groups=mesh['dp'=8,'seq'=4] {'dp'}, use_global_device_ids=true, to_apply=%region_37.38.clone | all-reduce | flops 3072 | bytes 18432
  806.7 9.8 %reduce-scatter.35.cloned.1.call-done = f32[96,2]{1,0:T(8,128)} async-done(((f32[768,2]{1,0:T(8,128)}), f32[96,2]{1,0:T(8,128)}) %reduce-scatter.35.cloned.1.call-update) | async-done | bytes 784
  823.2 30.0 %reduce-scatter.33.cloned.1.call-done = f32[96,6]{1,0:T(8,128)} async-done(((f32[768,6]{1,0:T(8,128)}), f32[96,6]{1,0:T(8,128)}) %reduce-scatter.33.cloned.1.call-update) | async-done | bytes 2320
  854.1 11.8 %all-reduce.1 = (bf16[384]{0:T(512)(128)(2,1)S(1)}, bf16[6,96]{1,0:T(8,128)(2,1)S(1)}, bf16[2,96]{1,0:T(2,128)(2,1)S(1)}) all-reduce(bf16[384]{0:T(512)(128)(2,1)S(1)} %dynamic-slice.5, bf16[6,96]{1,0:T(8,128)(2,1)S(1)} %copy.87, bf16[2,96]{1,0:T(2,128)(2,1)S(1)} %copy.89), channel_id=1, replica_groups=mesh['dp'=8,'seq'=4] {'seq'}, use_global_device_ids=true, to_apply=%region_38.39 | all-reduce | flops 1152 | bytes 4608 | tf_op jit(solution)/shard_map/psum | solution.py:302
  867.7 70.5 %all-reduce.5.cloned.1.call-done = (bf16[96,2304]{0,1:T(8,128)(2,1)}, bf16[96,768]{1,0:T(8,128)(2,1)}, bf16[96,3072]{1,0:T(8,128)(2,1)}, bf16[384,768]{1,0:T(8,128)(2,1)}) async-done(((bf16[96,2304]{0,1:T(8,128)(2,1)}, bf16[96,768]{1,0:T(8,128)(2,1)}, bf16[96,3072]{1,0:T(8,128)(2,1)}, bf16[384,768]{1,0:T(8,128)(2,1)}), (bf16[96,2304]{0,1:T(8,128)(2,1)}, bf16[96,768]{1,0:T(8,128)(2,1)}, ...) | async-done | bytes 1769488 | tf_op jit(solution)/shard_map/psum | solution.py:298
  (306 shorter events, 178.3 us)
Async XLA Ops:
  7.2 82.2 %copy-start = (s32[12,16,3]{1,2,0:T(4,128)S(1)}, s32[12,16,3]{1,2,0:T(4,128)}, u32[]{:S(2)}) copy-start(s32[12,16,3]{1,2,0:T(4,128)} %param.14) | copy-start | bytes 6916
  7.2 40.0 %all-gather.16.cloned.1.call-start = ((), (), s32[]{:S(2)}) async-start(), calls=%async_computation.10 | async-start | bytes 3981312 | tf_op jit(solution)/shard_map/all_gather | solution.py:263
  9.2 43.4 %copy-start.50 = (f32[6,96]{1,0:T(8,128)S(1)}, f32[6,96]{1,0:T(8,128)}, u32[]{:S(2)}) copy-start(f32[6,96]{1,0:T(8,128)} %param.20) | copy-start | bytes 6916
  9.3 52.5 %copy-start.19 = (bf16[2,1,256,768]{3,2,1,0:T(8,128)(2,1)S(1)}, bf16[2,1,256,768]{3,2,1,0:T(8,128)(2,1)}, u32[]{:S(2)}) copy-start(bf16[2,1,256,768]{3,2,1,0:T(8,128)(2,1)} %param.11) | copy-start | bytes 2359300
  9.3 104.4 %all-gather.30.cloned.1.call-start = ((), (), s32[]{:S(2)}) async-start(), calls=%async_computation.24 | async-start | bytes 1966080 | tf_op jit(solution)/shard_map/all_gather | solution.py:82
  52.6 76.6 %all-gather.28.cloned.1.call-start = ((), (), s32[]{:S(2)}) async-start(), calls=%async_computation.23 | async-start | bytes 1966080 | tf_op jit(solution)/shard_map/all_gather | solution.py:85
  66.3 86.4 %all-gather.18.cloned.1.call-start = ((), (), s32[]{:S(2)}) async-start(), calls=%async_computation.11 | async-start | bytes 1327104 | tf_op jit(solution)/shard_map/all_gather | solution.py:264
  67.1 126.9 %all-gather.20.cloned.1.call-start = ((), (), s32[]{:S(2)}) async-start(), calls=%async_computation.12 | async-start | bytes 5308416 | tf_op jit(solution)/shard_map/all_gather | solution.py:265
  69.3 165.9 %all-gather.22.cloned.1.call-start = ((), (), s32[]{:S(2)}) async-start(), calls=%async_computation.13 | async-start | bytes 5308416 | tf_op jit(solution)/shard_map/all_gather | solution.py:266
  71.6 202.9 %all-gather.26.cloned.1.call-start = ((), (), s32[]{:S(2)}) async-start(), calls=%async_computation.22 | async-start | bytes 1966080 | tf_op jit(solution)/shard_map/all_gather | solution.py:82
  72.4 240.2 %all-gather.24.cloned.1.call-start = ((), (), s32[]{:S(2)}) async-start(), calls=%async_computation.21 | async-start | bytes 1966080 | tf_op jit(solution)/shard_map/all_gather | solution.py:85
  113.3 164.0 %copy-start.17 = (bf16[256,768]{0,1:T(8,128)(2,1)}, bf16[256,768]{0,1:T(8,128)(2,1)S(1)}, u32[]{:S(2)}) copy-start(bf16[256,768]{0,1:T(8,128)(2,1)S(1)} %copy.75) | copy-start | bytes 1179652
  113.3 311.8 %reduce-scatter.19.cloned.1.call-start = ((), (), s32[]{:S(2)}) async-start(), calls=%async_computation.15 | async-start | bytes 1966080 | tf_op jit(solution)/shard_map/reduce_scatter | solution.py:200
  137.7 67.9 %copy-start.44 = (bf16[12,64,256]{2,1,0:T(8,128)(2,1)}, bf16[12,64,256]{2,1,0:T(8,128)(2,1)S(1)}, u32[]{:S(2)}) copy-start(bf16[12,64,256]{2,1,0:T(8,128)(2,1)S(1)} %fusion.38) | copy-start | bytes 1179652
  239.6 37.8 %copy-start.47 = (pred[256,1024]{1,0:T(8,128)(4,1)S(1)}, pred[256,1024]{1,0:T(8,128)(4,1)}, u32[]{:S(2)}) copy-start(pred[256,1024]{1,0:T(8,128)(4,1)} %copy-done.46) | copy-start | bytes 786436
  360.9 70.7 %reduce-scatter.17.cloned.1.call-start = ((), (), s32[]{:S(2)}) async-start(), calls=%async_computation.14 | async-start | bytes 1966080 | tf_op jit(solution)/shard_map/reduce_scatter | solution.py:194
  377.5 91.3 %reduce-scatter.23.cloned.1.call-start = ((), (), s32[]{:S(2)}) async-start(), calls=%async_computation.17 | async-start | bytes 1966080 | tf_op jit(solution)/shard_map/reduce_scatter | solution.py:200
  391.4 113.8 %reduce-scatter.21.cloned.1.call-start = ((), (), s32[]{:S(2)}) async-start(), calls=%async_computation.16 | async-start | bytes 1966080 | tf_op jit(solution)/shard_map/reduce_scatter | solution.py:194
  408.3 141.8 %reduce-scatter.25.cloned.1.call-start = ((), (), s32[]{:S(2)}) async-start(), calls=%async_computation.18 | async-start | bytes 2654208 | tf_op jit(solution)/shard_map/reduce_scatter | solution.py:290
  412.8 206.6 %reduce-scatter.31.cloned.1.call-start = ((), (), s32[]{:S(2)}) async-start(), calls=%async_computation.25 | async-start | bytes 7962624
  520.9 178.3 %reduce-scatter.27.cloned.1.call-start = ((), (), s32[]{:S(2)}) async-start(), calls=%async_computation.19 | async-start | bytes 10616832 | tf_op jit(solution)/shard_map/reduce_scatter | solution.py:291
  529.3 249.7 %reduce-scatter.29.cloned.1.call-start = ((), (), s32[]{:S(2)}) async-start(), calls=%async_computation.20 | async-start | bytes 10616832 | tf_op jit(solution)/shard_map/reduce_scatter | solution.py:292
  538.4 278.1 %reduce-scatter.35.cloned.1.call-start = ((), (), s32[]{:S(2)}) async-start(), calls=%async_computation.27 | async-start | bytes 442368
  539.9 313.4 %reduce-scatter.33.cloned.1.call-start = ((), (), s32[]{:S(2)}) async-start(), calls=%async_computation.26 | async-start | bytes 442368
  541.6 396.6 %all-reduce.5.cloned.1.call-start = ((), (), s32[]{:S(2)}) async-start(), calls=%async_computation.28 | async-start | bytes 3833856 | tf_op jit(solution)/shard_map/psum | solution.py:298
  551.7 229.6 %copy-start.53 = (u32[32]{0:T(128)S(1)}, u32[32]{0:T(128)}, u32[]{:S(2)}) copy-start(u32[32]{0:T(128)} %constant.157) | copy-start | bytes 388
  621.6 184.1 %copy-start.34 = (bf16[1,1,256,768]{3,2,1,0:T(8,128)(2,1)S(1)}, bf16[1,1,256,768]{3,2,1,0:T(8,128)(2,1)}, u32[]{:S(2)}) copy-start(bf16[1,1,256,768]{3,2,1,0:T(8,128)(2,1)} %get-tuple-element.112) | copy-start | bytes 1179652
  621.6 184.1 %copy-start.35 = (bf16[1,1,256,768]{3,2,1,0:T(8,128)(2,1)S(1)}, bf16[1,1,256,768]{3,2,1,0:T(8,128)(2,1)}, u32[]{:S(2)}) copy-start(bf16[1,1,256,768]{3,2,1,0:T(8,128)(2,1)} %get-tuple-element.113) | copy-start | bytes 1179652
  701.4 115.9 %copy-start.25 = (f32[256,768]{1,0:T(8,128)S(1)}, f32[256,768]{1,0:T(8,128)}, u32[]{:S(2)}) copy-start(f32[256,768]{1,0:T(8,128)} %get-tuple-element.121) | copy-start | bytes 2359300
  701.4 115.9 %copy-start.33 = (bf16[12,64,256]{2,1,0:T(8,128)(2,1)S(1)}, bf16[12,64,256]{2,1,0:T(8,128)(2,1)}, u32[]{:S(2)}) copy-start(bf16[12,64,256]{2,1,0:T(8,128)(2,1)} %get-tuple-element.147) | copy-start | bytes 1179652
  701.4 115.9 %copy-start.43 = (bf16[1,256,768]{1,2,0:T(8,128)(2,1)S(1)}, bf16[1,256,768]{1,2,0:T(8,128)(2,1)}, u32[]{:S(2)}) copy-start(bf16[1,256,768]{1,2,0:T(8,128)(2,1)} %reduce-scatter.21.cloned.1.call-done) | copy-start | bytes 1179652
  822.0 123.4 %copy-start.1 = (s32[12,16,3]{1,2,0:T(4,128)S(1)}, s32[12,16,3]{1,2,0:T(4,128)}, u32[]{:S(2)}) copy-start(s32[12,16,3]{1,2,0:T(4,128)} %param.14) | copy-start | bytes 6916
  (48 other events, 250.5 us)
Sparse Core Ops, SparseCore 0:
  10.5 36.6 all-gather.15
  52.8 37.0 all-gather.29
  92.0 35.9 all-gather.27
  129.8 22.9 all-gather.17
  155.0 38.9 all-gather.19
  196.3 38.9 all-gather.21
  237.4 37.0 all-gather.25
  276.6 35.9 all-gather.23
  361.0 34.1 reduce-scatter.18
  397.3 34.2 reduce-scatter.16
  434.5 34.2 reduce-scatter.22
  471.0 34.2 reduce-scatter.20
  508.6 41.4 reduce-scatter.24
  553.9 65.4 reduce-scatter.30
  622.7 76.4 reduce-scatter.26
  702.6 76.4 reduce-scatter.28
  782.6 33.8 reduce-scatter.34
  819.4 33.8 reduce-scatter.32
  856.4 81.6 all-reduce.4
where the time goes:
time: 959 us; the launch traced here: 952 us
  waiting for transfers between devices  597 us (62%)
  matrix products  162 us (17%)
  local copies, waits for them, and re-layouts  64.6 us (7%)
  blocking collectives  60.5 us (6%)
  other arithmetic  50 us (5%)
  between operations  16.1 us (2%)
    unnamed x22, waiting for transfers between devices  108 us
    reduce_scatter x1, waiting for transfers between devices, body(): lax.psum_scatter(totals[3], 'dp', scatter_dimension=0, tiled=True)  77.7 us
    reduce_scatter x1, waiting for transfers between devices, body(): lax.psum_scatter(totals[2], 'dp', scatter_dimension=0, tiled=True)  77.6 us
    psum x1, waiting for transfers between devices, body(): lax.psum(shards[0].astype(jnp.bfloat16), 'seq').astype(jnp.float32)  70.5 us
    reduce_scatter x2, waiting for transfers between devices, backward_pass(): lax.psum_scatter(key_part.reshape(seq_count, seq_len, model_width).astype...  42.9 us
    all_gather x1, waiting for transfers between devices, body(): lax.all_gather(halves[2], 'dp', axis=0, tiled=True)  39.1 us
    all_gather x1, waiting for transfers between devices, body(): lax.all_gather(halves[0], 'dp', axis=0, tiled=True)  37.9 us
    all_gather x2, waiting for transfers between devices, forward_pass(): lax.all_gather(keys_loc.reshape(seq_count, local_rows, model_width), 'seq...  35 us
  transfers between devices with their start and end apart: 19, of which 16 were waited for; matrix products, arithmetic and copies ran while one was open for 22% of the time, Pallas kernels for 0%

commit v1 on v0

--- a/solution.py
+++ b/solution.py
@@ -5,6 +5,27 @@
 
 EPSILON = 1e-05
 MASKED = -1e30
+
+
+def ring_gather(value, axis, dim):
+    size, place, rows = (lax.axis_size(axis), lax.axis_index(axis), value.shape[dim])
+    right = [(i, (i + 1) % size) for i in range(size)]
+    left = [(i, (i - 1) % size) for i in range(size)]
+    whole = jnp.zeros((*value.shape[:dim], size * rows, *value.shape[dim + 1 :]), value.dtype)
+    whole = lax.dynamic_update_slice_in_dim(whole, value, place * rows, axis=dim)
+    from_left = from_right = value
+    middle = size // 2
+    for step in range(1, middle + 1):
+        from_left = lax.ppermute(from_left, axis, right)
+        whole = lax.dynamic_update_slice_in_dim(
+            whole, from_left, (place - step) % size * rows, axis=dim
+        )
+        if step < size - middle:
+            from_right = lax.ppermute(from_right, axis, left)
+            whole = lax.dynamic_update_slice_in_dim(
+                whole, from_right, (place + step) % size * rows, axis=dim
+            )
+    return whole
 
 
 def layer_norm(tensor, gain_row, offset):
@@ -82,9 +103,7 @@
         lax.all_gather(
             keys_loc.reshape(seq_count, local_rows, model_width), "seq", axis=1, tiled=True
         ),
-        lax.all_gather(
-            values_loc.reshape(seq_count, local_rows, model_width), "seq", axis=1, tiled=True
-        ),
+        ring_gather(values_loc.reshape(seq_count, local_rows, model_width), "seq", 1),
     )
     seq_len = keys_full.shape[1]
     query_heads = queries.reshape(seq_count, local_rows, head_count, head_size)

time: 959 us -> 914 us (0.953)
  waiting for transfers between devices: 597 us -> 532 us
  local copies, waits for them, and re-layouts: 64.6 us -> 85.4 us
    all_gather x1, waiting for transfers between devices: 39.1 us -> 4.62 us  [body(): lax.all_gather(halves[2], 'dp', axis=0, tiled=True)]
    all_gather x2 -> x0, waiting for transfers between devices: 24 us -> none  [forward_pass(): lax.all_gather(values_loc.reshape(seq_count, local_rows, model_width), 's...]
    all_gather x1, waiting for transfers between devices: 15 us -> 0.01 us  [body(): lax.all_gather(halves[1], 'dp', axis=0, tiled=True)]
    ppermute x0 -> x6, local copies, waits for them, and re-layouts: none -> 11.5 us  [the longest x4 7.66 us: ring_gather(): from_left = lax.ppermute(from_left, axis, right)]
    unnamed x132 -> x136, local copies, waits for them, and re-layouts: 28.7 us -> 31.3 us
    unnamed x22 -> x20, waiting for transfers between devices: 108 us -> 108 us
  transfers between devices with their start and end apart: 19 -> 23, of which waited for: 16 -> 16; matrix products, arithmetic and copies ran while one was open for 22% -> 23% of each run, Pallas kernels for 0% -> 0%
where the time goes in v1:
time: 914 us; the launch traced here: 906 us
  waiting for transfers between devices  532 us (58%)
  matrix products  155 us (17%)
  local copies, waits for them, and re-layouts  85.4 us (9%)
  blocking collectives  60.4 us (7%)
  other arithmetic  48.2 us (5%)
  between operations  16.4 us (2%)
    unnamed x20, waiting for transfers between devices  108 us
    reduce_scatter x1, waiting for transfers between devices, body(): lax.psum_scatter(totals[2], 'dp', scatter_dimension=0, tiled=True)  77.8 us
    reduce_scatter x1, waiting for transfers between devices, body(): lax.psum_scatter(totals[3], 'dp', scatter_dimension=0, tiled=True)  77.7 us
    psum x1, waiting for transfers between devices, body(): lax.psum(shards[0].astype(jnp.bfloat16), 'seq').astype(jnp.float32)  70.4 us
    reduce_scatter x2, waiting for transfers between devices, backward_pass(): lax.psum_scatter(key_part.reshape(seq_count, seq_len, model_width).astype...  43.3 us
    all_gather x1, waiting for transfers between devices, body(): lax.all_gather(halves[0], 'dp', axis=0, tiled=True)  37.9 us
    all_gather x2, waiting for transfers between devices, forward_pass(): lax.all_gather(keys_loc.reshape(seq_count, local_rows, model_width), 'seq...  34 us
    dot_general x8, matrix products, outer_grad(): lax.dot_general(left, right, (((0,), (0,)), ((), ())), preferred_element_...  33.4 us
  transfers between devices with their start and end apart: 23, of which 16 were waited for; matrix products, arithmetic and copies ran while one was open for 23% of the time, Pallas kernels for 0%

profile of v1, /device:TPU:0, one launch (start us, length us, event | category | flops | bytes accessed | tf_op | source)
XLA Modules:
  0.0 905.5 jit_solution(15123889313823833585)
XLA Ops:
  9.3 37.9 %all-gather.12.cloned.1.call-done = bf16[768,2304]{1,0:T(8,128)(2,1)} async-done(((bf16[96,2304]{1,0:T(8,128)(2,1)}), bf16[768,2304]{1,0:T(8,128)(2,1)}) %all-gather.12.cloned.1.call-update) | async-done | bytes 3538960 | tf_op jit(solution)/shard_map/all_gather | solution.py:282
  55.4 8.9 all-gather.2
  64.4 7.8 all-gather.3
  85.4 8.9 all-gather.4
  98.7 17.3 %reshape.625 = pred[12,256,1024]{2,1,0:T(32,128)(4,1)} reshape(pred[12,4,64,16,64]{4,3,2,1,0:T(8,128)(4,1)} %broadcast_in_dim.25) | data formatting | bytes 6291456 | tf_op jit(solution)/shard_map/reshape | solution.py:78
  153.2 6.4 fusion.102
  174.8 11.6 %multiply_convert_fusion.4 = (bf16[256,3072]{1,0:T(8,128)(2,1)}, f32[256,3072]{1,0:T(8,128)}, f32[256,3072]{1,0:T(8,128)}) fusion(f32[3072]{0:T(1024)S(1)} %bitcast.243, bf16[768,3072]{1,0:T(8,128)(2,1)} %all-gather.16.cloned.1.call-done, f32[256,768]{1,0:T(8,128)S(1)} %get-tuple-element.135, f32[256]{0:T(256)S(1)} %fusion.81, ...), kind=kOutput, calls=%fused_computation.37 | convolution fusion | flops 1260847104 | bytes 13389824 | tf_op jit(solution)/shard_map/dot_general | solution.py:130
  186.4 29.6 %all-gather.18.cloned.1.call-done = bf16[3072,768]{1,0:T(8,128)(2,1)} async-done(((bf16[384,768]{1,0:T(8,128)(2,1)}), bf16[3072,768]{1,0:T(8,128)(2,1)}) %all-gather.18.cloned.1.call-update) | async-done | bytes 4718608 | tf_op jit(solution)/shard_map/all_gather | solution.py:285
  220.7 34.0 %all-gather.20.cloned.1.call-done = bf16[1024,768]{1,0:T(8,128)(2,1)} async-done(((bf16[256,768]{1,0:T(8,128)(2,1)}), bf16[1024,768]{1,0:T(8,128)(2,1)}) %all-gather.20.cloned.1.call-update) | async-done | bytes 1572880 | tf_op jit(solution)/shard_map/all_gather | solution.py:103
  257.2 6.7 fusion.99
  274.2 11.0 %multiply_convert_fusion.5 = (bf16[256,3072]{1,0:T(8,128)(2,1)S(1)}, f32[256,3072]{1,0:T(8,128)}, f32[256,3072]{1,0:T(8,128)}) fusion(f32[3072]{0:T(1024)S(1)} %bitcast.244, bf16[768,3072]{1,0:T(8,128)(2,1)S(1)} %bitcast.248, f32[256,768]{1,0:T(8,128)S(1)} %get-tuple-element.128, f32[768]{0:T(1024)S(1)} %get-tuple-element.70, ...), kind=kOutput, calls=%fused_computation.50 | convolution fusion | flops 1260847104 | bytes 13389824 | tf_op jit(solution)/shard_map/dot_general | solution.py:130
  305.8 8.1 fusion.24
  314.0 7.0 multiply_reduce_fusion.1
  321.0 6.4 multiply_convert_fusion.1
  336.3 8.0 fusion.27
  344.4 7.2 multiply_reduce_fusion
  351.6 6.6 multiply_convert_fusion
  366.1 6.2 convert_reduce_fusion.7
  378.0 6.9 reduce-scatter.17.cloned.1.call-done
  390.1 31.9 %reduce-scatter.23.cloned.1.call-done = bf16[1,256,768]{1,2,0:T(8,128)(2,1)} async-done(((bf16[1,1024,768]{1,2,0:T(8,128)(2,1)}), bf16[1,256,768]{1,2,0:T(8,128)(2,1)}) %reduce-scatter.23.cloned.1.call-update) | async-done | bytes 393232 | tf_op jit(solution)/shard_map/reduce_scatter | solution.py:219
  422.0 36.4 %reduce-scatter.21.cloned.1.call-done = bf16[1,256,768]{1,2,0:T(8,128)(2,1)} async-done(((bf16[1,1024,768]{1,2,0:T(8,128)(2,1)}), bf16[1,256,768]{1,2,0:T(8,128)(2,1)}) %reduce-scatter.21.cloned.1.call-update) | async-done | bytes 393232 | tf_op jit(solution)/shard_map/reduce_scatter | solution.py:213
  458.5 7.4 add_bitcast_fusion
  465.8 8.2 copy.112
  494.9 8.4 reduce-scatter.25.cloned.1.call-done
  504.9 67.7 %reduce-scatter.31.cloned.1.call-done = f32[96,2304]{1,0:T(8,128)} async-done(((f32[768,2304]{1,0:T(8,128)}), f32[96,2304]{1,0:T(8,128)}) %reduce-scatter.31.cloned.1.call-update) | async-done | bytes 884752
  574.8 77.8 %reduce-scatter.27.cloned.1.call-done = f32[96,3072]{1,0:T(8,128)} async-done(((f32[768,3072]{1,0:T(8,128)}), f32[96,3072]{1,0:T(8,128)}) %reduce-scatter.27.cloned.1.call-update) | async-done | bytes 1179664 | tf_op jit(solution)/shard_map/reduce_scatter | solution.py:310
  654.8 77.7 %reduce-scatter.29.cloned.1.call-done = f32[384,768]{1,0:T(8,128)} async-done(((f32[3072,768]{1,0:T(8,128)}), f32[384,768]{1,0:T(8,128)}) %reduce-scatter.29.cloned.1.call-update) | async-done | bytes 1179664 | tf_op jit(solution)/shard_map/reduce_scatter | solution.py:311
  735.9 23.1 %all-reduce = bf16[3072]{0:T(1024)(128)(2,1)S(1)} all-reduce(f32[3072]{0:T(1024)S(1)} %add.377), channel_id=12, replica_groups=mesh['dp'=8,'seq'=4] {'dp'}, use_global_device_ids=true, to_apply=%region_37.38.clone | all-reduce | flops 3072 | bytes 18432
  760.1 9.8 %reduce-scatter.35.cloned.1.call-done = f32[96,2]{1,0:T(8,128)} async-done(((f32[768,2]{1,0:T(8,128)}), f32[96,2]{1,0:T(8,128)}) %reduce-scatter.35.cloned.1.call-update) | async-done | bytes 784
  776.6 30.0 %reduce-scatter.33.cloned.1.call-done = f32[96,6]{1,0:T(8,128)} async-done(((f32[768,6]{1,0:T(8,128)}), f32[96,6]{1,0:T(8,128)}) %reduce-scatter.33.cloned.1.call-update) | async-done | bytes 2320
  807.5 11.8 %all-reduce.1 = (bf16[384]{0:T(512)(128)(2,1)S(1)}, bf16[6,96]{1,0:T(8,128)(2,1)S(1)}, bf16[2,96]{1,0:T(2,128)(2,1)S(1)}) all-reduce(bf16[384]{0:T(512)(128)(2,1)S(1)} %dynamic-slice.5, bf16[6,96]{1,0:T(8,128)(2,1)S(1)} %copy.115, bf16[2,96]{1,0:T(2,128)(2,1)S(1)} %copy.117), channel_id=1, replica_groups=mesh['dp'=8,'seq'=4] {'seq'}, use_global_device_ids=true, to_apply=%region_38.39 | all-reduce | flops 1152 | bytes 4608 | tf_op jit(solution)/shard_map/psum | solution.py:321
  821.0 70.4 %all-reduce.5.cloned.1.call-done = (bf16[96,2304]{0,1:T(8,128)(2,1)}, bf16[96,768]{1,0:T(8,128)(2,1)}, bf16[96,3072]{1,0:T(8,128)(2,1)}, bf16[384,768]{1,0:T(8,128)(2,1)}) async-done(((bf16[96,2304]{0,1:T(8,128)(2,1)}, bf16[96,768]{1,0:T(8,128)(2,1)}, bf16[96,3072]{1,0:T(8,128)(2,1)}, bf16[384,768]{1,0:T(8,128)(2,1)}), (bf16[96,2304]{0,1:T(8,128)(2,1)}, bf16[96,768]{1,0:T(8,128)(2,1)}, ...) | async-done | bytes 1769488 | tf_op jit(solution)/shard_map/psum | solution.py:317
  (331 shorter events, 192.3 us)
Async XLA Ops:
  7.2 65.1 %copy-start = (s32[12,16,3]{1,2,0:T(4,128)S(1)}, s32[12,16,3]{1,2,0:T(4,128)}, u32[]{:S(2)}) copy-start(s32[12,16,3]{1,2,0:T(4,128)} %param.14) | copy-start | bytes 6916
  7.2 40.0 %all-gather.12.cloned.1.call-start = ((), (), s32[]{:S(2)}) async-start(), calls=%async_computation.10 | async-start | bytes 3981312 | tf_op jit(solution)/shard_map/all_gather | solution.py:282
  9.3 44.2 %copy-start.42 = (f32[96,3072]{1,0:T(8,128)S(1)}, f32[96,3072]{1,0:T(8,128)}, u32[]{:S(2)}) copy-start(f32[96,3072]{1,0:T(8,128)} %param.17) | copy-start | bytes 3538948
  9.3 141.7 %all-gather.22.cloned.1.call-start = ((), (), s32[]{:S(2)}) async-start(), calls=%async_computation.22 | async-start | bytes 1966080 | tf_op jit(solution)/shard_map/all_gather | solution.py:103
  52.7 115.3 %all-gather.14.cloned.1.call-start = ((), (), s32[]{:S(2)}) async-start(), calls=%async_computation.11 | async-start | bytes 1327104 | tf_op jit(solution)/shard_map/all_gather | solution.py:283
  53.4 121.4 %all-gather.16.cloned.1.call-start = ((), (), s32[]{:S(2)}) async-start(), calls=%async_computation.12 | async-start | bytes 5308416 | tf_op jit(solution)/shard_map/all_gather | solution.py:284
  54.4 161.7 %all-gather.18.cloned.1.call-start = ((), (), s32[]{:S(2)}) async-start(), calls=%async_computation.13 | async-start | bytes 5308416 | tf_op jit(solution)/shard_map/all_gather | solution.py:285
  55.3 199.3 %all-gather.20.cloned.1.call-start = ((), (), s32[]{:S(2)}) async-start(), calls=%async_computation.21 | async-start | bytes 1966080 | tf_op jit(solution)/shard_map/all_gather | solution.py:103
  79.3 43.5 %collective-permute-start.3 = (bf16[1,256,768]{2,1,0:T(8,128)(2,1)}, bf16[1,256,768]{2,1,0:T(8,128)(2,1)}, u32[]{:S(2)}, u32[]{:S(2)}) collective-permute-start(bf16[1,256,768]{2,1,0:T(8,128)(2,1)} %get-tuple-element.110), channel_id=1, source_target_pairs={{0,1},{1,2},{2,3},{3,0},{4,5},{5,6},{6,7},{7,4},{8,9},{9,10},{10,1... | collective-permute-start | bytes 1179656 | tf_op jit(solution)/shard_map/ppermute | solution.py:19
  80.8 45.5 %collective-permute-start = (bf16[1,256,768]{2,1,0:T(8,128)(2,1)}, bf16[1,256,768]{2,1,0:T(8,128)(2,1)}, u32[]{:S(2)}, u32[]{:S(2)}) collective-permute-start(bf16[1,256,768]{2,1,0:T(8,128)(2,1)} %get-tuple-element.116), channel_id=1, source_target_pairs={{0,1},{1,2},{2,3},{3,0},{4,5},{5,6},{6,7},{7,4},{8,9},{9,10},{10,1... | collective-permute-start | bytes 1179656 | tf_op jit(solution)/shard_map/ppermute | solution.py:19
  82.4 46.9 %collective-permute-start.4 = (bf16[1,256,768]{2,1,0:T(8,128)(2,1)}, bf16[1,256,768]{2,1,0:T(8,128)(2,1)}, u32[]{:S(2)}, u32[]{:S(2)}) collective-permute-start(bf16[1,256,768]{2,1,0:T(8,128)(2,1)} %get-tuple-element.110), channel_id=1, source_target_pairs={{0,3},{1,0},{2,1},{3,2},{4,7},{5,4},{6,5},{7,6},{8,11},{9,8},{10,9... | collective-permute-start | bytes 1179656 | tf_op jit(solution)/shard_map/ppermute | solution.py:24
  84.8 46.5 %collective-permute-start.1 = (bf16[1,256,768]{2,1,0:T(8,128)(2,1)}, bf16[1,256,768]{2,1,0:T(8,128)(2,1)}, u32[]{:S(2)}, u32[]{:S(2)}) collective-permute-start(bf16[1,256,768]{2,1,0:T(8,128)(2,1)} %get-tuple-element.116), channel_id=1, source_target_pairs={{0,3},{1,0},{2,1},{3,2},{4,7},{5,4},{6,5},{7,6},{8,11},{9,8},{10,9... | collective-permute-start | bytes 1179656 | tf_op jit(solution)/shard_map/ppermute | solution.py:24
  121.7 256.3 %reduce-scatter.19.cloned.1.call-start = ((), (), s32[]{:S(2)}) async-start(), calls=%async_computation.15 | async-start | bytes 1966080 | tf_op jit(solution)/shard_map/reduce_scatter | solution.py:219
  124.7 14.1 %collective-permute-start.5 = (bf16[1,256,768]{2,1,0:T(8,128)(2,1)}, bf16[1,256,768]{2,1,0:T(8,128)(2,1)}, u32[]{:S(2)}, u32[]{:S(2)}) collective-permute-start(bf16[1,256,768]{2,1,0:T(8,128)(2,1)} %collective-permute-done.3), channel_id=1, source_target_pairs={{0,1},{1,2},{2,3},{3,0},{4,5},{5,6},{6,7},{7,4},{8,9},{9,10},{10,1... | collective-permute-start | bytes 1179656 | tf_op jit(solution)/shard_map/ppermute | solution.py:19
  126.2 20.4 %collective-permute-start.2 = (bf16[1,256,768]{2,1,0:T(8,128)(2,1)}, bf16[1,256,768]{2,1,0:T(8,128)(2,1)}, u32[]{:S(2)}, u32[]{:S(2)}) collective-permute-start(bf16[1,256,768]{2,1,0:T(8,128)(2,1)} %collective-permute-done), channel_id=1, source_target_pairs={{0,1},{1,2},{2,3},{3,0},{4,5},{5,6},{6,7},{7,4},{8,9},{9,10},{10,1... | collective-permute-start | bytes 1179656 | tf_op jit(solution)/shard_map/ppermute | solution.py:19
  313.9 70.9 %reduce-scatter.17.cloned.1.call-start = ((), (), s32[]{:S(2)}) async-start(), calls=%async_computation.14 | async-start | bytes 1966080 | tf_op jit(solution)/shard_map/reduce_scatter | solution.py:213
  330.5 91.5 %reduce-scatter.23.cloned.1.call-start = ((), (), s32[]{:S(2)}) async-start(), calls=%async_computation.17 | async-start | bytes 1966080 | tf_op jit(solution)/shard_map/reduce_scatter | solution.py:219
  344.3 114.1 %reduce-scatter.21.cloned.1.call-start = ((), (), s32[]{:S(2)}) async-start(), calls=%async_computation.16 | async-start | bytes 1966080 | tf_op jit(solution)/shard_map/reduce_scatter | solution.py:213
  361.3 141.9 %reduce-scatter.25.cloned.1.call-start = ((), (), s32[]{:S(2)}) async-start(), calls=%async_computation.18 | async-start | bytes 2654208 | tf_op jit(solution)/shard_map/reduce_scatter | solution.py:309
  365.8 206.8 %reduce-scatter.31.cloned.1.call-start = ((), (), s32[]{:S(2)}) async-start(), calls=%async_computation.23 | async-start | bytes 7962624
  474.1 178.5 %reduce-scatter.27.cloned.1.call-start = ((), (), s32[]{:S(2)}) async-start(), calls=%async_computation.19 | async-start | bytes 10616832 | tf_op jit(solution)/shard_map/reduce_scatter | solution.py:310
  482.6 249.9 %reduce-scatter.29.cloned.1.call-start = ((), (), s32[]{:S(2)}) async-start(), calls=%async_computation.20 | async-start | bytes 10616832 | tf_op jit(solution)/shard_map/reduce_scatter | solution.py:311
  491.6 278.2 %reduce-scatter.35.cloned.1.call-start = ((), (), s32[]{:S(2)}) async-start(), calls=%async_computation.25 | async-start | bytes 442368
  493.1 313.5 %reduce-scatter.33.cloned.1.call-start = ((), (), s32[]{:S(2)}) async-start(), calls=%async_computation.24 | async-start | bytes 442368
  494.9 396.5 %all-reduce.5.cloned.1.call-start = ((), (), s32[]{:S(2)}) async-start(), calls=%async_computation.26 | async-start | bytes 3833856 | tf_op jit(solution)/shard_map/psum | solution.py:317
  504.9 229.8 %copy-start.54 = (u32[32]{0:T(128)S(1)}, u32[32]{0:T(128)}, u32[]{:S(2)}) copy-start(u32[32]{0:T(128)} %constant.190) | copy-start | bytes 388
  574.8 184.3 %copy-start.35 = (bf16[1,1,256,768]{3,2,1,0:T(8,128)(2,1)S(1)}, bf16[1,1,256,768]{3,2,1,0:T(8,128)(2,1)}, u32[]{:S(2)}) copy-start(bf16[1,1,256,768]{3,2,1,0:T(8,128)(2,1)} %get-tuple-element.112) | copy-start | bytes 1179652
  574.8 184.3 %copy-start.36 = (bf16[1,1,256,768]{3,2,1,0:T(8,128)(2,1)S(1)}, bf16[1,1,256,768]{3,2,1,0:T(8,128)(2,1)}, u32[]{:S(2)}) copy-start(bf16[1,1,256,768]{3,2,1,0:T(8,128)(2,1)} %get-tuple-element.113) | copy-start | bytes 1179652
  654.8 115.9 %copy-start.26 = (f32[256,768]{1,0:T(8,128)S(1)}, f32[256,768]{1,0:T(8,128)}, u32[]{:S(2)}) copy-start(f32[256,768]{1,0:T(8,128)} %get-tuple-element.121) | copy-start | bytes 2359300
  654.8 115.9 %copy-start.34 = (bf16[12,64,256]{2,1,0:T(8,128)(2,1)S(1)}, bf16[12,64,256]{2,1,0:T(8,128)(2,1)}, u32[]{:S(2)}) copy-start(bf16[12,64,256]{2,1,0:T(8,128)(2,1)} %get-tuple-element.147) | copy-start | bytes 1179652
  654.8 115.9 %copy-start.47 = (bf16[1,256,768]{1,2,0:T(8,128)(2,1)S(1)}, bf16[1,256,768]{1,2,0:T(8,128)(2,1)}, u32[]{:S(2)}) copy-start(bf16[1,256,768]{1,2,0:T(8,128)(2,1)} %reduce-scatter.21.cloned.1.call-done) | copy-start | bytes 1179652
  775.3 123.2 %copy-start.1 = (s32[12,16,3]{1,2,0:T(4,128)S(1)}, s32[12,16,3]{1,2,0:T(4,128)}, u32[]{:S(2)}) copy-start(s32[12,16,3]{1,2,0:T(4,128)} %param.14) | copy-start | bytes 6916
  (54 other events, 377.0 us)
Sparse Core Ops, SparseCore 0:
  10.5 36.6 all-gather.11
  52.8 56.1 all-gather.21
  110.9 22.6 all-gather.13
  135.9 38.9 all-gather.15
  177.1 38.9 all-gather.17
  217.5 37.0 all-gather.19
  314.0 34.1 reduce-scatter.18
  350.5 34.2 reduce-scatter.16
  387.7 34.2 reduce-scatter.22
  424.2 34.2 reduce-scatter.20
  461.8 41.4 reduce-scatter.24
  507.0 65.4 reduce-scatter.30
  576.1 76.4 reduce-scatter.26
  656.0 76.4 reduce-scatter.28
  736.0 33.8 reduce-scatter.34
  772.7 33.8 reduce-scatter.32
  809.7 81.6 all-reduce.4
